TPU v7x, 32 devices: a whole 2x2x4 slice. The times are simulated.
32 devices in a mesh: seq: 8 (over z, y), mp: 4 (over x, core).
Axes of the slice: x: 2, y: 2, z: 4, core: 2. Of those that a mesh axis runs over, the one named last changes fastest.
Arguments:
- incoming_image_patches: bfloat16 [1, 128, 128, 1152], P(None, 'seq', 'mp'), may hold values from -6 to 6
- initial_standardize_scaling: float32 [1152], replicated, may hold values from 0.1 to 1.9
- acceptance_matrix: bfloat16 [1152, 1024], P(None, 'mp'), may hold values from -0.1875 to 0.1875
- addressing_matrix: bfloat16 [1152, 1024], P(None, 'mp'), may hold values from -0.1875 to 0.1875
- content_matrix: bfloat16 [1152, 1024], P(None, 'mp'), may hold values from -0.1875 to 0.1875
- forgetting_lowdim_left_factor: bfloat16 [1152, 64], replicated, may hold values from -0.1875 to 0.1875
- forgetting_lowdim_right_factor: bfloat16 [64, 1024], P(None, 'mp'), may hold values from -1.5 to 1.5
- forgetting_baseline: float32 [1024], P('mp'), may hold values from -6 to 1
- self_token_reward: float32 [1024], P('mp'), may hold values from -3 to 3
- horizontal_cluster_scaling: float32 [1024], P('mp'), may hold values from 0.1 to 1.9
- vertical_cluster_scaling: float32 [1024], P('mp'), may hold values from 0.1 to 1.9
- temporal_mix_projection_matrix: bfloat16 [1024, 1152], P('mp'), may hold values from -0.1875 to 0.1875
- later_standardize_scaling: float32 [1152], replicated, may hold values from 0.1 to 1.9
- feature_mix_addressing_matrix: bfloat16 [1152, 4608], P('seq', 'mp'), may hold values from -0.1875 to 0.1875
- feature_mix_content_matrix: bfloat16 [4608, 1152], P('mp', 'seq'), may hold values from -0.09375 to 0.09375
Outputs:
- block_out: bfloat16 [1, 128, 128, 1152], P(None, 'seq', 'mp')
All inputs are finite; a program needn't handle non-finite values.
Results may differ from a plain program's by a relative error of at most 0.017.
Values may be sent and summed in bfloat16 or wider, within the bound.
A program may use at most 128 MiB of HBM per device.

v0:
```python
import jax
import jax.numpy as jnp
from jax import lax
from jax.sharding import PartitionSpec as P

SUBSPACE_SIZE = 64


def layer_norm(inputs, gain):
    values = inputs.astype(jnp.float32)
    average = jnp.mean(values, axis=-1, keepdims=True)
    centred = values - average
    spread = jnp.mean(centred * centred, axis=-1, keepdims=True)
    return (centred * lax.rsqrt(spread + 1e-05) * gain).astype(jnp.bfloat16)


def heads_first(array, nheads):
    number, length, inner_width = array.shape
    shaped = array.astype(jnp.float32).reshape(number, length, nheads, inner_width // nheads)
    return shaped.transpose(0, 2, 1, 3)


def recurrence(recept_in, keying_in, decays_in, valued_in, boost_in, gain):
    number, length, inner_width = recept_in.shape
    nheads = inner_width // SUBSPACE_SIZE
    head_size = inner_width // nheads
    blocks = length // 16
    acceptance_horizontal_lines = heads_first(recept_in, nheads)
    addressing_horizontal_lines = heads_first(keying_in, nheads)
    decays = heads_first(decays_in, nheads)
    content_horizontal_lines = heads_first(valued_in, nheads)
    boost = boost_in.reshape(nheads, 1, head_size)
    running = jnp.cumsum(decays, axis=2)
    before = running - decays
    before_blocks = before.reshape(number, nheads, blocks, 16, head_size)
    anchor = before_blocks[:, :, :, :1, :]
    queries = acceptance_horizontal_lines.reshape(number, nheads, blocks, 16, head_size) * jnp.exp(
        before_blocks - anchor
    )
    places = jnp.arange(length)
    limits = (jnp.arange(blocks) + 1) * 16
    usable = places[None, :] < limits[:, None]
    exponent = anchor - running[:, :, None, :, :]
    exponent = jnp.where(usable[None, None, :, :, None], exponent, -10000.0)
    weighted = addressing_horizontal_lines[:, :, None, :, :] * jnp.exp(exponent)
    scores = jnp.einsum("nhbqc,nhbsc->nhbqs", queries, weighted, precision=lax.Precision.HIGHEST)
    query_places = places.reshape(blocks, 16)
    earlier = places[None, None, :] < query_places[:, :, None]
    scores = jnp.where(earlier[None, None], scores, 0.0)
    current = jnp.sum(acceptance_horizontal_lines * boost * addressing_horizontal_lines, axis=-1)
    summed = jnp.einsum(
        "nhbqs,nhsc->nhbqc", scores, content_horizontal_lines, precision=lax.Precision.HIGHEST
    )
    summed = (
        summed.reshape(number, nheads, length, head_size)
        + current[..., None] * content_horizontal_lines
    )
    average = jnp.mean(summed, axis=-1, keepdims=True)
    centred = summed - average
    spread = jnp.mean(centred * centred, axis=-1, keepdims=True)
    normed = (
        (centred * lax.rsqrt(spread + 0.00064))
        .transpose(0, 2, 1, 3)
        .reshape(number, length, inner_width)
    )
    return (normed * gain).astype(jnp.bfloat16)


def lines_of_columns(array):
    images, height, columns, inner_width = array.shape
    return jnp.swapaxes(array, 1, 2).reshape(images * columns, height, inner_width)


def shards(
    incoming_image_patches,
    initial_standardize_scaling,
    acceptance_matrix,
    addressing_matrix,
    content_matrix,
    forgetting_lowdim_left_factor,
    forgetting_lowdim_right_factor,
    forgetting_baseline,
    self_token_reward,
    horizontal_cluster_scaling,
    vertical_cluster_scaling,
    temporal_mix_projection_matrix,
    later_standardize_scaling,
    feature_mix_addressing_matrix,
    feature_mix_content_matrix,
):
    images, row_count, part_cols, model_width = incoming_image_patches.shape
    whole_rows = lax.all_gather(incoming_image_patches, "mp", axis=2, tiled=True)
    full_cols = whole_rows.shape[2]
    inner_width = acceptance_matrix.shape[1]
    grid_shape = (images, row_count, full_cols, inner_width)
    xn1 = layer_norm(whole_rows, initial_standardize_scaling).reshape(-1, model_width)
    acceptance_horizontal_lines = jnp.dot(
        xn1, acceptance_matrix, preferred_element_type=jnp.float32
    ).astype(jnp.bfloat16)
    addressing_horizontal_lines = jnp.dot(
        xn1, addressing_matrix, preferred_element_type=jnp.float32
    ).astype(jnp.bfloat16)
    content_horizontal_lines = jnp.dot(
        xn1, content_matrix, preferred_element_type=jnp.float32
    ).astype(jnp.bfloat16)
    latent = jnp.tanh(
        jnp.dot(xn1, forgetting_lowdim_left_factor, preferred_element_type=jnp.float32)
    ).astype(jnp.bfloat16)
    forgetting_log_amount = (
        -0.7
        * jax.nn.sigmoid(
            forgetting_baseline
            + jnp.dot(latent, forgetting_lowdim_right_factor, preferred_element_type=jnp.float32)
        )
    ).astype(jnp.bfloat16)
    recept_grid = acceptance_horizontal_lines.reshape(grid_shape)
    keying_grid = addressing_horizontal_lines.reshape(grid_shape)
    decay_grid = forgetting_log_amount.reshape(grid_shape)
    line_shape = (images * row_count, full_cols, inner_width)
    horizontal_recurrence_result = recurrence(
        acceptance_horizontal_lines.reshape(line_shape),
        addressing_horizontal_lines.reshape(line_shape),
        forgetting_log_amount.reshape(line_shape),
        content_horizontal_lines.reshape(line_shape),
        self_token_reward,
        horizontal_cluster_scaling,
    )
    col_recept, col_keying, col_decay, col_valued = (
        lax.all_to_all(recept_grid, "seq", split_axis=2, concat_axis=1, tiled=True),
        lax.all_to_all(keying_grid, "seq", split_axis=2, concat_axis=1, tiled=True),
        lax.all_to_all(decay_grid, "seq", split_axis=2, concat_axis=1, tiled=True),
        lax.all_to_all(
            horizontal_recurrence_result.reshape(grid_shape),
            "seq",
            split_axis=2,
            concat_axis=1,
            tiled=True,
        ),
    )
    height = col_recept.shape[1]
    columns = col_recept.shape[2]
    vertical_recurrence_result = recurrence(
        lines_of_columns(col_recept),
        lines_of_columns(col_keying),
        lines_of_columns(col_decay),
        lines_of_columns(col_valued),
        self_token_reward,
        vertical_cluster_scaling,
    )
    back_grid = jnp.swapaxes(
        vertical_recurrence_result.reshape(images, columns, height, inner_width), 1, 2
    )
    row_grid = lax.all_to_all(back_grid, "seq", split_axis=1, concat_axis=2, tiled=True)
    partial_value = jnp.dot(
        row_grid.reshape(-1, inner_width),
        temporal_mix_projection_matrix,
        preferred_element_type=jnp.float32,
    )
    partial_value = lax.optimization_barrier(partial_value.astype(jnp.bfloat16)).astype(jnp.float32)
    partial_value = partial_value.reshape(images, row_count, full_cols, model_width)
    totals = lax.psum(partial_value.astype(jnp.bfloat16), "mp").astype(jnp.float32)
    residual_all = (whole_rows.astype(jnp.float32) + totals).astype(jnp.bfloat16)
    mix_input = layer_norm(residual_all, later_standardize_scaling)
    residual = lax.dynamic_slice_in_dim(
        residual_all, lax.axis_index("mp") * part_cols, part_cols, 2
    )
    flattened = mix_input.reshape(-1, model_width)
    hidden_pre = jnp.dot(
        flattened,
        lax.all_gather(feature_mix_addressing_matrix, "seq", axis=0, tiled=True),
        preferred_element_type=jnp.float32,
    )
    positive = jnp.maximum(hidden_pre, 0.0)
    hidden = (positive * positive).astype(jnp.bfloat16)
    downward = jnp.dot(
        hidden,
        lax.all_gather(feature_mix_content_matrix, "seq", axis=1, tiled=True),
        preferred_element_type=jnp.float32,
    )
    downward = lax.optimization_barrier(downward.astype(jnp.bfloat16)).astype(jnp.float32)
    downward = downward.reshape(images, row_count, full_cols, model_width)
    mixed = lax.psum_scatter(
        downward.astype(jnp.bfloat16), "mp", scatter_dimension=2, tiled=True
    ).astype(jnp.float32)
    return (residual.astype(jnp.float32) + mixed).astype(jnp.bfloat16)


def solution(mesh):
    placed = (
        P(None, "seq", "mp", None),
        P(),
        P(None, "mp"),
        P(None, "mp"),
        P(None, "mp"),
        P(),
        P(None, "mp"),
        P("mp"),
        P("mp"),
        P("mp"),
        P("mp"),
        P("mp", None),
        P(),
        P("seq", "mp"),
        P("mp", "seq"),
    )
    return jax.shard_map(
        shards, mesh=mesh, in_specs=placed, out_specs=P(None, "seq", "mp", None), check_vma=False
    )
```

profile of v0, /device:TPU:0, one launch (start us, length us, event | category | flops | bytes accessed | tf_op | source)
XLA Modules:
  0.0 550.7 jit_solution(13070111403937969308)
XLA Ops:
  9.0 40.9 %all-gather.4.cloned.1.call-done = bf16[1,16,128,1152]{3,2,1,0:T(8,128)(2,1)} async-done(((bf16[1,16,32,1152]{3,2,1,0:T(8,128)(2,1)}), bf16[1,16,128,1152]{3,2,1,0:T(8,128)(2,1)}) %all-gather.4.cloned.1.call-update) | async-done | bytes 4718608 | tf_op jit(solution)/shard_map/all_gather | solution.py:92
  63.9 4.9 copy.216
  68.8 4.8 copy.187
  73.7 4.5 fusion.54
  81.3 8.0 %bitcast_subtract_fusion = (f32[16,4,128,64]{3,0,1,2:T(8,128)S(1)}, f32[16,4,128,64]{3,0,1,2:T(8,128)}) fusion(f32[16,128,4,64]{3,2,1,0:T(4,128)} %reshape.302), kind=kOutput, calls=%fused_computation.42 | output fusion | flops 67108864 | bytes 6291456 | tf_op jit(solution)/shard_map/jit(cumsum)/reduce_window_sum | solution.py:33
  91.4 4.8 copy.196
  108.3 5.7 %convolution_convert_fusion.2 = bf16[2048,256]{1,0:T(8,128)(2,1)} fusion(bf16[2048,1152]{1,0:T(8,128)(2,1)} %bitcast.152, bf16[1152,256]{1,0:T(8,128)(2,1)} %param.19), kind=kOutput, calls=%fused_computation.66 | convolution fusion | flops 1208483840 | bytes 6356992 | tf_op jit(solution)/shard_map/dot_general | solution.py:103
  117.8 22.1 %fusion.1 = f32[16,4,8,16,128]{4,3,2,1,0:T(8,128)S(1)} fusion(f32[16,4,128,64]{2,3,1,0:T(8,128)} %copy.196, f32[16,4,8,64]{3,2,1,0:T(8,128)S(1)} %copy.191, f32[16,4,128,64]{2,3,1,0:T(8,128)S(1)} %bitcast.135, pred[8,128]{1,0:T(8,128)(4,1)S(1)} %iota_compare_fusion.1, f32[16,4,8,16,64]{4,3,2,1,0:T(8,128)} %bitcast.161, f32[16,4,8,16,64]{4,0,1,3,2:T(8,128)} %bitcast.147), kind=kOutput, calls=%fused_computation.1 | convolution fusion | flops 818937856 | bytes 12715008 | tf_op jit(solution)/shard_map/nhbqc,nhbsc->nhbqs/dot_general | solution.py:46
  156.3 5.6 %all-to-all-start.3 = ((bf16[1,16,128,256]{3,1,0,2:T(8,128)(2,1)}), bf16[1,16,128,256]{3,1,0,2:T(8,128)(2,1)}, u32[]{:S(2)}, u32[]{:S(2)}) async-start(bf16[1,16,128,256]{3,1,0,2:T(8,128)(2,1)} %multiply_convert_fusion.1), calls=%async_computation.3 | async-start | bytes 2097152 | tf_op jit(solution)/shard_map/all_to_all | solution.py:132
  164.8 23.4 %all-to-all-done.3 = bf16[1,16,128,256]{3,1,0,2:T(8,128)(2,1)} async-done(((bf16[1,16,128,256]{3,1,0,2:T(8,128)(2,1)}), bf16[1,16,128,256]{3,1,0,2:T(8,128)(2,1)}, u32[]{:S(2)}, u32[]{:S(2)}) %all-to-all-start.3) | async-done | bytes 1048608 | tf_op jit(solution)/shard_map/all_to_all | solution.py:132
  188.2 4.2 all-to-all-start.1
  194.0 24.0 %all-to-all-done.1 = bf16[1,16,128,256]{3,1,0,2:T(8,128)(2,1)} async-done(((bf16[1,16,128,256]{3,1,0,2:T(8,128)(2,1)}), bf16[1,16,128,256]{3,1,0,2:T(8,128)(2,1)}, u32[]{:S(2)}, u32[]{:S(2)}) %all-to-all-start.1) | async-done | bytes 1048608 | tf_op jit(solution)/shard_map/all_to_all | solution.py:131
  223.2 24.2 %all-to-all-done = bf16[1,16,128,256]{3,1,0,2:T(8,128)(2,1)S(1)} async-done(((bf16[1,16,128,256]{3,1,0,2:T(8,128)(2,1)}), bf16[1,16,128,256]{3,1,0,2:T(8,128)(2,1)S(1)}, u32[]{:S(2)}, u32[]{:S(2)}) %all-to-all-start) | async-done | bytes 1048608 | tf_op jit(solution)/shard_map/all_to_all | solution.py:129
  247.5 4.2 all-to-all-start.2
  260.5 4.6 copy.177
  265.1 6.1 %bitcast_subtract_fusion.1 = (f32[16,4,128,64]{3,0,1,2:T(8,128)S(1)}, f32[16,4,128,64]{3,0,1,2:T(8,128)}) fusion(f32[16,128,4,64]{3,0,2,1:T(8,128)} %copy.177), kind=kOutput, calls=%fused_computation.45 | output fusion | flops 67108864 | bytes 6291456 | tf_op jit(solution)/shard_map/jit(cumsum)/reduce_window_sum | solution.py:33
  273.4 4.7 copy.185
  291.5 22.4 %fusion.6 = f32[16,4,8,16,128]{4,3,2,1,0:T(8,128)S(1)} fusion(f32[16,4,128,64]{2,3,1,0:T(8,128)} %copy.185, f32[16,4,8,64]{3,2,1,0:T(8,128)S(1)} %copy.178, f32[16,4,128,64]{2,3,1,0:T(8,128)} %bitcast.140, pred[8,128]{1,0:T(8,128)(4,1)S(1)} %iota_compare_fusion.1, f32[16,4,8,16,64]{4,3,2,1,0:T(8,128)} %bitcast.160, f32[16,4,8,16,64]{4,0,1,3,2:T(8,128)} %bitcast.145), kind=kOutput, calls=%fused_computation.6 | convolution fusion | flops 818937856 | bytes 12715008 | tf_op jit(solution)/shard_map/nhbqc,nhbsc->nhbqs/dot_general | solution.py:46
  330.0 30.6 %all_to_all.69 = bf16[1,128,16,256]{3,2,0,1:T(8,128)(2,1)S(1)} all-to-all(bf16[1,128,16,256]{3,2,0,1:T(8,128)(2,1)S(1)} %fusion.68), channel_id=1, replica_groups=mesh['seq'=8,'mp'=4] {'seq'}, dimensions={1} | all-to-all | bytes 2097152 | tf_op jit(solution)/shard_map/all_to_all | solution.py:153
  365.7 91.0 %all-reduce.2.cloned.1.call-done = bf16[1,16,128,1152]{3,2,1,0:T(8,128)(2,1)} async-done(((bf16[1,16,128,1152]{3,2,1,0:T(8,128)(2,1)}), bf16[1,16,128,1152]{3,2,1,0:T(8,128)(2,1)}) %all-reduce.2.cloned.1.call-update) | async-done | bytes 4718608 | tf_op jit(solution)/shard_map/psum | solution.py:161
  456.6 5.3 convert_reduce_fusion.1
  467.3 8.3 %all-gather.8.cloned.1.call-done = bf16[1152,1152]{0,1:T(8,128)(2,1)} async-done(((bf16[1152,144]{0,1:T(8,128)(2,1)}), bf16[1152,1152]{0,1:T(8,128)(2,1)}) %all-gather.8.cloned.1.call-update) | async-done | bytes 2654224 | tf_op jit(solution)/shard_map/all_gather | solution.py:177
  475.5 18.4 %convolution_convert_fusion = bf16[2048,1152]{1,0:T(8,128)(2,1)} fusion(bf16[1152,1152]{0,1:T(8,128)(2,1)} %all-gather.8.cloned.1.call-done, bf16[2048,1152]{1,0:T(8,128)(2,1)} %bitcast.153, bf16[1152,1152]{1,0:T(8,128)(2,1)} %all-gather.6.cloned.1.call-done), kind=kOutput, calls=%fused_computation.40 | convolution fusion | flops 10881073152 | bytes 14745600 | tf_op jit(solution)/shard_map/dot_general | solution.py:175
  493.9 46.6 %reduce-scatter.2.cloned.1.call-done = bf16[1,16,32,1152]{3,2,1,0:T(8,128)(2,1)} async-done(((bf16[1,16,128,1152]{3,2,1,0:T(8,128)(2,1)}), bf16[1,16,32,1152]{3,2,1,0:T(8,128)(2,1)}) %reduce-scatter.2.cloned.1.call-update) | async-done | bytes 1179664 | tf_op jit(solution)/shard_map/reduce_scatter | solution.py:182
  (135 shorter events, 116.1 us)
Async XLA Ops:
  7.4 353.3 %copy-start = (bf16[256,1152]{1,0:T(8,128)(2,1)S(1)}, bf16[256,1152]{1,0:T(8,128)(2,1)}, u32[]{:S(2)}) copy-start(bf16[256,1152]{1,0:T(8,128)(2,1)} %param.26) | copy-start | bytes 1769476
  7.4 42.5 %all-gather.4.cloned.1.call-start = ((), (), s32[]{:S(2)}) async-start(), calls=%async_computation.6 | async-start | bytes 5898240 | tf_op jit(solution)/shard_map/all_gather | solution.py:92
  9.0 46.1 %copy-start.17 = (f32[1152]{0:T(1024)S(1)}, f32[1152]{0:T(1024)}, u32[]{:S(2)}) copy-start(f32[1152]{0:T(1024)} %param.16) | copy-start | bytes 13828
  60.8 8.0 %copy-start.10 = (bf16[2048,256]{1,0:T(8,128)(2,1)}, bf16[2048,256]{1,0:T(8,128)(2,1)S(1)}, u32[]{:S(2)}) copy-start(bf16[2048,256]{1,0:T(8,128)(2,1)S(1)} %convolution_convert_fusion.4) | copy-start | bytes 3145732
  68.8 4.8 copy-start.23
  68.8 4.8 copy-start.24
  68.8 4.8 copy-start.25
  78.1 11.1 %copy-start.14 = (bf16[2048,256]{1,0:T(8,128)(2,1)}, bf16[2048,256]{1,0:T(8,128)(2,1)S(1)}, u32[]{:S(2)}) copy-start(bf16[2048,256]{1,0:T(8,128)(2,1)S(1)} %fusion.54) | copy-start | bytes 3145732
  89.3 7.0 %copy-start.22 = (bf16[1152,256]{1,0:T(8,128)(2,1)S(1)}, bf16[1152,256]{1,0:T(8,128)(2,1)}, u32[]{:S(2)}) copy-start(bf16[1152,256]{1,0:T(8,128)(2,1)} %param.18) | copy-start | bytes 1769476
  108.3 9.5 %copy-start.6 = (f32[16,128,4,64]{1,3,2,0:T(8,128)}, f32[16,128,4,64]{1,3,2,0:T(8,128)S(1)}, u32[]{:S(2)}) copy-start(f32[16,128,4,64]{1,3,2,0:T(8,128)S(1)} %copy.194) | copy-start | bytes 6291460
  117.8 22.1 %copy-start.3 = (bf16[32,8,16,128]{3,2,1,0:T(8,128)(2,1)}, bf16[32,8,16,128]{3,2,1,0:T(8,128)(2,1)S(1)}, u32[]{:S(2)}) copy-start(bf16[32,8,16,128]{3,2,1,0:T(8,128)(2,1)S(1)} %copy.223) | copy-start | bytes 3145732
  156.3 36.2 %copy-start.11 = (bf16[2048,256]{1,0:T(8,128)(2,1)S(1)}, bf16[2048,256]{1,0:T(8,128)(2,1)}, u32[]{:S(2)}) copy-start(bf16[2048,256]{1,0:T(8,128)(2,1)} %copy-done.10) | copy-start | bytes 3145732
  156.3 31.9 %all-to-all-start.3 = ((bf16[1,16,128,256]{3,1,0,2:T(8,128)(2,1)}), bf16[1,16,128,256]{3,1,0,2:T(8,128)(2,1)}, u32[]{:S(2)}, u32[]{:S(2)}) async-start(bf16[1,16,128,256]{3,1,0,2:T(8,128)(2,1)} %multiply_convert_fusion.1), calls=%async_computation.3 | async-start | bytes 2097152 | tf_op jit(solution)/shard_map/all_to_all | solution.py:132
  161.9 59.7 %copy-start.13 = (bf16[2048,256]{1,0:T(8,128)(2,1)S(1)}, bf16[2048,256]{1,0:T(8,128)(2,1)}, u32[]{:S(2)}) copy-start(bf16[2048,256]{1,0:T(8,128)(2,1)} %copy-done.12) | copy-start | bytes 3145732
  188.2 29.8 %all-to-all-start.1 = ((bf16[1,16,128,256]{3,1,0,2:T(8,128)(2,1)}), bf16[1,16,128,256]{3,1,0,2:T(8,128)(2,1)}, u32[]{:S(2)}, u32[]{:S(2)}) async-start(bf16[1,16,128,256]{3,1,0,2:T(8,128)(2,1)} %copy.173), calls=%async_computation.1 | async-start | bytes 2097152 | tf_op jit(solution)/shard_map/all_to_all | solution.py:131
  218.1 29.4 %all-to-all-start = ((bf16[1,16,128,256]{3,1,0,2:T(8,128)(2,1)}), bf16[1,16,128,256]{3,1,0,2:T(8,128)(2,1)S(1)}, u32[]{:S(2)}, u32[]{:S(2)}) async-start(bf16[1,16,128,256]{3,1,0,2:T(8,128)(2,1)} %copy.168), calls=%async_computation | async-start | bytes 2097152 | tf_op jit(solution)/shard_map/all_to_all | solution.py:129
  247.5 7.7 %copy-start.15 = (bf16[1,16,128,256]{3,1,0,2:T(8,128)(2,1)}, bf16[1,16,128,256]{3,1,0,2:T(8,128)(2,1)S(1)}, u32[]{:S(2)}) copy-start(bf16[1,16,128,256]{3,1,0,2:T(8,128)(2,1)S(1)} %all-to-all-done) | copy-start | bytes 3145732
  247.5 37.7 %all-to-all-start.2 = ((bf16[1,16,128,256]{3,1,0,2:T(8,128)(2,1)}), bf16[1,16,128,256]{3,1,0,2:T(8,128)(2,1)}, u32[]{:S(2)}, u32[]{:S(2)}) async-start(bf16[1,16,128,256]{3,1,0,2:T(8,128)(2,1)} %copy.180), calls=%async_computation.2 | async-start | bytes 2097152 | tf_op jit(solution)/shard_map/all_to_all | solution.py:130
  251.7 204.9 %all-reduce.2.cloned.1.call-start = ((), (), s32[]{:S(2)}) async-start(), calls=%async_computation.7 | async-start | bytes 9437184 | tf_op jit(solution)/shard_map/psum | solution.py:161
  271.2 7.0 %copy-start.16 = (bf16[1,16,128,256]{3,1,0,2:T(8,128)(2,1)S(1)}, bf16[1,16,128,256]{3,1,0,2:T(8,128)(2,1)}, u32[]{:S(2)}) copy-start(bf16[1,16,128,256]{3,1,0,2:T(8,128)(2,1)} %copy-done.15) | copy-start | bytes 3145732
  291.5 22.4 %copy-start.5 = (bf16[1,16,128,256]{2,3,1,0:T(8,128)(2,1)S(1)}, bf16[1,16,128,256]{2,3,1,0:T(8,128)(2,1)}, u32[]{:S(2)}) copy-start(bf16[1,16,128,256]{2,3,1,0:T(8,128)(2,1)} %copy.204) | copy-start | bytes 3145732
  364.4 102.8 %all-gather.6.cloned.1.call-start = ((), (), s32[]{:S(2)}) async-start(), calls=%async_computation.8 | async-start | bytes 2985984 | tf_op jit(solution)/shard_map/all_gather | solution.py:170
  365.0 110.5 %all-gather.8.cloned.1.call-start = ((), (), s32[]{:S(2)}) async-start(), calls=%async_computation.9 | async-start | bytes 2985984 | tf_op jit(solution)/shard_map/all_gather | solution.py:177
  365.6 174.9 %reduce-scatter.2.cloned.1.call-start = ((), (), s32[]{:S(2)}) async-start(), calls=%async_computation.10 | async-start | bytes 5898240 | tf_op jit(solution)/shard_map/reduce_scatter | solution.py:182
  (11 other events, 28.9 us)
Sparse Core Ops, SparseCore 0:
  9.7 40.1 all-gather.3
  364.6 92.0 all-reduce.1
  494.0 46.4 reduce-scatter.1
Sparse Core Ops, SparseCore 1:
  367.1 52.9 all-gather.5
  422.1 53.4 all-gather.7
where the time goes:
time: 554 us; the launch traced here: 551 us
  waiting for transfers between devices  260 us (47%)
  local copies, waits for them, and re-layouts  89.8 us (16%)
  matrix products  89.8 us (16%)
  other arithmetic  47.2 us (9%)
  blocking collectives  30.6 us (6%)
  starting transfers between devices  17.9 us (3%)
  between operations  15.3 us (3%)
    psum x1, waiting for transfers between devices, shards(): lax.psum(partial_value.astype(jnp.bfloat16), 'mp').astype(jnp.float32)  91 us
    reduce_scatter x1, waiting for transfers between devices, shards(): lax.psum_scatter(downward.astype(jnp.bfloat16), 'mp', scatter_dimension=2...  46.6 us
    dot_general x2, matrix products, recurrence(): jnp.einsum('nhbqc,nhbsc->nhbqs', queries, weighted, precision=lax.Precisi...  44.5 us
    transpose x14, local copies, waits for them, and re-layouts, heads_first(): return shaped.transpose(0, 2, 1, 3)  42.1 us
    all_gather x1, waiting for transfers between devices, shards(): lax.all_gather(incoming_image_patches, 'mp', axis=2, tiled=True)  40.9 us
    all_to_all x1, blocking collectives, shards(): lax.all_to_all(back_grid, 'seq', split_axis=1, concat_axis=2, tiled=True)  30.6 us
    all_to_all x1, waiting for transfers between devices, shards(): lax.all_to_all(recept_grid, 'seq', split_axis=2, concat_axis=1, tiled=True)  24.2 us
    all_to_all x1, waiting for transfers between devices, shards(): lax.all_to_all(decay_grid, 'seq', split_axis=2, concat_axis=1, tiled=True)  24 us
  transfers between devices with their start and end apart: 9, of which 7 were waited for; matrix products, arithmetic and copies ran while one was open for 9% of the time, Pallas kernels for 0%

commit v1 on v0

--- a/solution.py
+++ b/solution.py
@@ -158,7 +158,9 @@
     )
     partial_value = lax.optimization_barrier(partial_value.astype(jnp.bfloat16)).astype(jnp.float32)
     partial_value = partial_value.reshape(images, row_count, full_cols, model_width)
-    totals = lax.psum(partial_value.astype(jnp.bfloat16), "mp").astype(jnp.float32)
+    totals = jnp.sum(lax.all_gather(partial_value.astype(jnp.bfloat16), "mp"), axis=0).astype(
+        jnp.float32
+    )
     residual_all = (whole_rows.astype(jnp.float32) + totals).astype(jnp.bfloat16)
     mix_input = layer_norm(residual_all, later_standardize_scaling)
     residual = lax.dynamic_slice_in_dim(

time: 554 us -> 672 us (1.21)
  waiting for transfers between devices: 260 us -> 366 us
  other arithmetic: 47.2 us -> 60.9 us
    all_gather x0 -> x1, waiting for transfers between devices: none -> 117 us  [shards(): lax.all_gather(partial_value.astype(jnp.bfloat16), 'mp')]
    psum x1 -> x0, waiting for transfers between devices: 91 us -> none  [shards(): lax.psum(partial_value.astype(jnp.bfloat16), 'mp').astype(jnp.float32)]
    all_gather x1, waiting for transfers between devices: 0.01 us -> 55.6 us  [shards(): lax.all_gather(feature_mix_addressing_matrix, 'seq', axis=0, tiled=True)]
    all_gather x1, waiting for transfers between devices: 8.25 us -> 32.9 us  [shards(): lax.all_gather(feature_mix_content_matrix, 'seq', axis=1, tiled=True)]
    reduce_sum x0 -> x1, other arithmetic: none -> 13.9 us  [shards(): jnp.sum(lax.all_gather(partial_value.astype(jnp.bfloat16), 'mp'), axis=0)]
  transfers between devices with their start and end apart: 9 -> 9, of which waited for: 7 -> 8; matrix products, arithmetic and copies ran while one was open for 9% -> 9% of each run, Pallas kernels for 0% -> 0%
where the time goes in v1:
time: 672 us; the launch traced here: 668 us
  waiting for transfers between devices  366 us (54%)
  matrix products  89.6 us (13%)
  local copies, waits for them, and re-layouts  89.1 us (13%)
  other arithmetic  60.9 us (9%)
  blocking collectives  30.6 us (5%)
  starting transfers between devices  17.8 us (3%)
  between operations  13.9 us (2%)
    all_gather x1, waiting for transfers between devices, shards(): lax.all_gather(partial_value.astype(jnp.bfloat16), 'mp')  117 us
    all_gather x1, waiting for transfers between devices, shards(): lax.all_gather(feature_mix_addressing_matrix, 'seq', axis=0, tiled=True)  55.6 us
    reduce_scatter x1, waiting for transfers between devices, shards(): lax.psum_scatter(downward.astype(jnp.bfloat16), 'mp', scatter_dimension=2...  46.6 us
    dot_general x2, matrix products, recurrence(): jnp.einsum('nhbqc,nhbsc->nhbqs', queries, weighted, precision=lax.Precisi...  44.4 us
    transpose x14, local copies, waits for them, and re-layouts, heads_first(): return shaped.transpose(0, 2, 1, 3)  41.5 us
    all_gather x1, waiting for transfers between devices, shards(): lax.all_gather(incoming_image_patches, 'mp', axis=2, tiled=True)  40.9 us
    all_gather x1, waiting for transfers between devices, shards(): lax.all_gather(feature_mix_content_matrix, 'seq', axis=1, tiled=True)  32.9 us
    all_to_all x1, blocking collectives, shards(): lax.all_to_all(back_grid, 'seq', split_axis=1, concat_axis=2, tiled=True)  30.6 us
  transfers between devices with their start and end apart: 9, of which 8 were waited for; matrix products, arithmetic and copies ran while one was open for 9% of the time, Pallas kernels for 0%

profile of v1, /device:TPU:0, one launch (start us, length us, event | category | flops | bytes accessed | tf_op | source)
XLA Modules:
  0.0 668.4 jit_solution(6357435187911256981)
XLA Ops:
  8.2 40.9 %all-gather.5.cloned.1.call-done = bf16[1,16,128,1152]{3,2,1,0:T(8,128)(2,1)} async-done(((bf16[1,16,32,1152]{3,2,1,0:T(8,128)(2,1)}), bf16[1,16,128,1152]{3,2,1,0:T(8,128)(2,1)}) %all-gather.5.cloned.1.call-update) | async-done | bytes 4718608 | tf_op jit(solution)/shard_map/all_gather | solution.py:92
  63.3 4.8 copy.216
  68.1 4.8 copy.187
  73.0 4.5 fusion.54
  80.7 8.0 %bitcast_subtract_fusion = (f32[16,4,128,64]{3,0,1,2:T(8,128)S(1)}, f32[16,4,128,64]{3,0,1,2:T(8,128)}) fusion(f32[16,128,4,64]{3,2,1,0:T(4,128)} %reshape.315), kind=kOutput, calls=%fused_computation.42 | output fusion | flops 67108864 | bytes 6291456 | tf_op jit(solution)/shard_map/jit(cumsum)/reduce_window_sum | solution.py:33
  90.8 4.8 copy.196
  107.2 5.7 convolution_convert_fusion.2
  116.7 22.1 %fusion.1 = f32[16,4,8,16,128]{4,3,2,1,0:T(8,128)S(1)} fusion(f32[16,4,128,64]{2,3,1,0:T(8,128)} %copy.196, f32[16,4,8,64]{3,2,1,0:T(8,128)S(1)} %copy.191, f32[16,4,128,64]{2,3,1,0:T(8,128)S(1)} %bitcast.139, pred[8,128]{1,0:T(8,128)(4,1)S(1)} %iota_compare_fusion.1, f32[16,4,8,16,64]{4,3,2,1,0:T(8,128)} %bitcast.165, f32[16,4,8,16,64]{4,0,1,3,2:T(8,128)} %bitcast.151), kind=kOutput, calls=%fused_computation.1 | convolution fusion | flops 818937856 | bytes 12715008 | tf_op jit(solution)/shard_map/nhbqc,nhbsc->nhbqs/dot_general | solution.py:46
  155.3 5.6 all-to-all-start.3
  163.8 23.4 %all-to-all-done.3 = bf16[1,16,128,256]{3,1,0,2:T(8,128)(2,1)} async-done(((bf16[1,16,128,256]{3,1,0,2:T(8,128)(2,1)}), bf16[1,16,128,256]{3,1,0,2:T(8,128)(2,1)}, u32[]{:S(2)}, u32[]{:S(2)}) %all-to-all-start.3) | async-done | bytes 1048608 | tf_op jit(solution)/shard_map/all_to_all | solution.py:132
  193.1 24.0 %all-to-all-done.1 = bf16[1,16,128,256]{3,1,0,2:T(8,128)(2,1)} async-done(((bf16[1,16,128,256]{3,1,0,2:T(8,128)(2,1)}), bf16[1,16,128,256]{3,1,0,2:T(8,128)(2,1)}, u32[]{:S(2)}, u32[]{:S(2)}) %all-to-all-start.1) | async-done | bytes 1048608 | tf_op jit(solution)/shard_map/all_to_all | solution.py:131
  222.2 24.2 %all-to-all-done = bf16[1,16,128,256]{3,1,0,2:T(8,128)(2,1)S(1)} async-done(((bf16[1,16,128,256]{3,1,0,2:T(8,128)(2,1)}), bf16[1,16,128,256]{3,1,0,2:T(8,128)(2,1)S(1)}, u32[]{:S(2)}, u32[]{:S(2)}) %all-to-all-start) | async-done | bytes 1048608 | tf_op jit(solution)/shard_map/all_to_all | solution.py:129
  259.5 4.5 copy.177
  264.0 6.1 bitcast_subtract_fusion.1
  272.2 4.7 copy.185
  290.1 22.3 %fusion.6 = f32[16,4,8,16,128]{4,3,2,1,0:T(8,128)S(1)} fusion(f32[16,4,128,64]{2,3,1,0:T(8,128)} %copy.185, f32[16,4,8,64]{3,2,1,0:T(8,128)S(1)} %copy.178, f32[16,4,128,64]{2,3,1,0:T(8,128)} %bitcast.144, pred[8,128]{1,0:T(8,128)(4,1)S(1)} %iota_compare_fusion.1, f32[16,4,8,16,64]{4,3,2,1,0:T(8,128)} %bitcast.164, f32[16,4,8,16,64]{4,0,1,3,2:T(8,128)} %bitcast.149), kind=kOutput, calls=%fused_computation.6 | convolution fusion | flops 818937856 | bytes 12715008 | tf_op jit(solution)/shard_map/nhbqc,nhbsc->nhbqs/dot_general | solution.py:46
  328.2 30.6 %all_to_all.69 = bf16[1,128,16,256]{3,2,0,1:T(8,128)(2,1)S(1)} all-to-all(bf16[1,128,16,256]{3,2,0,1:T(8,128)(2,1)S(1)} %fusion.68), channel_id=1, replica_groups=mesh['seq'=8,'mp'=4] {'seq'}, dimensions={1} | all-to-all | bytes 2097152 | tf_op jit(solution)/shard_map/all_to_all | solution.py:153
  364.1 116.8 %all-gather.7.cloned.1.call-done = bf16[4,1,16,128,1152]{4,3,2,1,0:T(8,128)(2,1)} async-done(((bf16[1,1,16,128,1152]{4,3,2,1,0:T(8,128)(2,1)}), bf16[4,1,16,128,1152]{4,3,2,1,0:T(8,128)(2,1)}) %all-gather.7.cloned.1.call-update) | async-done | bytes 18874384 | tf_op jit(solution)/shard_map/all_gather | solution.py:161
  480.9 13.9 %reduce_sum.110 = bf16[16,128,1152]{2,1,0:T(8,128)(2,1)} reduce(bf16[4,1,16,128,1152]{4,3,2,1,0:T(8,128)(2,1)} %all-gather.7.cloned.1.call-done, bf16[]{:T(256)} %constant.41.clone.1), dimensions={0,1}, to_apply=%region_10.11 | reduce | flops 7077888 | bytes 23592962 | tf_op jit(solution)/shard_map/reduce_sum | solution.py:161
  494.8 5.3 convert_reduce_fusion.1
  505.2 32.9 %all-gather.11.cloned.1.call-done = bf16[1152,1152]{0,1:T(8,128)(2,1)} async-done(((bf16[1152,144]{0,1:T(8,128)(2,1)}), bf16[1152,1152]{0,1:T(8,128)(2,1)}) %all-gather.11.cloned.1.call-update) | async-done | bytes 2654224 | tf_op jit(solution)/shard_map/all_gather | solution.py:179
  538.1 55.6 %all-gather.9.cloned.1.call-done = bf16[1152,1152]{1,0:T(8,128)(2,1)} async-done(((bf16[144,1152]{1,0:T(8,128)(2,1)}), bf16[1152,1152]{1,0:T(8,128)(2,1)}) %all-gather.9.cloned.1.call-update) | async-done | bytes 2654224 | tf_op jit(solution)/shard_map/all_gather | solution.py:172
  593.7 18.4 %convolution_convert_fusion = bf16[2048,1152]{1,0:T(8,128)(2,1)} fusion(bf16[1152,1152]{0,1:T(8,128)(2,1)} %all-gather.11.cloned.1.call-done, bf16[2048,1152]{1,0:T(8,128)(2,1)} %bitcast.157, bf16[1152,1152]{1,0:T(8,128)(2,1)} %all-gather.9.cloned.1.call-done), kind=kOutput, calls=%fused_computation.40 | convolution fusion | flops 10881073152 | bytes 14745600 | tf_op jit(solution)/shard_map/dot_general | solution.py:177
  612.1 46.6 %reduce-scatter.2.cloned.1.call-done = bf16[1,16,32,1152]{3,2,1,0:T(8,128)(2,1)} async-done(((bf16[1,16,128,1152]{3,2,1,0:T(8,128)(2,1)}), bf16[1,16,32,1152]{3,2,1,0:T(8,128)(2,1)}) %reduce-scatter.2.cloned.1.call-update) | async-done | bytes 1179664 | tf_op jit(solution)/shard_map/reduce_scatter | solution.py:184
  (136 shorter events, 124.0 us)
Async XLA Ops:
  6.5 352.4 %copy-start = (bf16[256,1152]{1,0:T(8,128)(2,1)S(1)}, bf16[256,1152]{1,0:T(8,128)(2,1)}, u32[]{:S(2)}) copy-start(bf16[256,1152]{1,0:T(8,128)(2,1)} %param.26) | copy-start | bytes 1769476
  6.5 42.5 %all-gather.5.cloned.1.call-start = ((), (), s32[]{:S(2)}) async-start(), calls=%async_computation.6 | async-start | bytes 5898240 | tf_op jit(solution)/shard_map/all_gather | solution.py:92
  8.2 46.1 %copy-start.17 = (f32[1152]{0:T(1024)S(1)}, f32[1152]{0:T(1024)}, u32[]{:S(2)}) copy-start(f32[1152]{0:T(1024)} %param.16) | copy-start | bytes 13828
  60.1 8.0 %copy-start.10 = (bf16[2048,256]{1,0:T(8,128)(2,1)}, bf16[2048,256]{1,0:T(8,128)(2,1)S(1)}, u32[]{:S(2)}) copy-start(bf16[2048,256]{1,0:T(8,128)(2,1)S(1)} %convolution_convert_fusion.4) | copy-start | bytes 3145732
  68.1 4.8 copy-start.23
  68.1 4.8 copy-start.24
  68.1 4.8 copy-start.25
  77.4 11.2 %copy-start.14 = (bf16[2048,256]{1,0:T(8,128)(2,1)}, bf16[2048,256]{1,0:T(8,128)(2,1)S(1)}, u32[]{:S(2)}) copy-start(bf16[2048,256]{1,0:T(8,128)(2,1)S(1)} %fusion.54) | copy-start | bytes 3145732
  88.6 7.0 %copy-start.22 = (bf16[1152,256]{1,0:T(8,128)(2,1)S(1)}, bf16[1152,256]{1,0:T(8,128)(2,1)}, u32[]{:S(2)}) copy-start(bf16[1152,256]{1,0:T(8,128)(2,1)} %param.18) | copy-start | bytes 1769476
  107.2 9.5 %copy-start.6 = (f32[16,128,4,64]{1,3,2,0:T(8,128)}, f32[16,128,4,64]{1,3,2,0:T(8,128)S(1)}, u32[]{:S(2)}) copy-start(f32[16,128,4,64]{1,3,2,0:T(8,128)S(1)} %copy.194) | copy-start | bytes 6291460
  116.7 22.1 %copy-start.3 = (bf16[32,8,16,128]{3,2,1,0:T(8,128)(2,1)}, bf16[32,8,16,128]{3,2,1,0:T(8,128)(2,1)S(1)}, u32[]{:S(2)}) copy-start(bf16[32,8,16,128]{3,2,1,0:T(8,128)(2,1)S(1)} %copy.223) | copy-start | bytes 3145732
  155.3 36.2 %copy-start.11 = (bf16[2048,256]{1,0:T(8,128)(2,1)S(1)}, bf16[2048,256]{1,0:T(8,128)(2,1)}, u32[]{:S(2)}) copy-start(bf16[2048,256]{1,0:T(8,128)(2,1)} %copy-done.10) | copy-start | bytes 3145732
  155.3 31.9 %all-to-all-start.3 = ((bf16[1,16,128,256]{3,1,0,2:T(8,128)(2,1)}), bf16[1,16,128,256]{3,1,0,2:T(8,128)(2,1)}, u32[]{:S(2)}, u32[]{:S(2)}) async-start(bf16[1,16,128,256]{3,1,0,2:T(8,128)(2,1)} %multiply_convert_fusion.1), calls=%async_computation.3 | async-start | bytes 2097152 | tf_op jit(solution)/shard_map/all_to_all | solution.py:132
  161.0 59.7 %copy-start.13 = (bf16[2048,256]{1,0:T(8,128)(2,1)S(1)}, bf16[2048,256]{1,0:T(8,128)(2,1)}, u32[]{:S(2)}) copy-start(bf16[2048,256]{1,0:T(8,128)(2,1)} %copy-done.12) | copy-start | bytes 3145732
  187.2 29.8 %all-to-all-start.1 = ((bf16[1,16,128,256]{3,1,0,2:T(8,128)(2,1)}), bf16[1,16,128,256]{3,1,0,2:T(8,128)(2,1)}, u32[]{:S(2)}, u32[]{:S(2)}) async-start(bf16[1,16,128,256]{3,1,0,2:T(8,128)(2,1)} %copy.173), calls=%async_computation.1 | async-start | bytes 2097152 | tf_op jit(solution)/shard_map/all_to_all | solution.py:131
  217.1 29.4 %all-to-all-start = ((bf16[1,16,128,256]{3,1,0,2:T(8,128)(2,1)}), bf16[1,16,128,256]{3,1,0,2:T(8,128)(2,1)S(1)}, u32[]{:S(2)}, u32[]{:S(2)}) async-start(bf16[1,16,128,256]{3,1,0,2:T(8,128)(2,1)} %copy.168), calls=%async_computation | async-start | bytes 2097152 | tf_op jit(solution)/shard_map/all_to_all | solution.py:129
  246.5 7.7 %copy-start.15 = (bf16[1,16,128,256]{3,1,0,2:T(8,128)(2,1)}, bf16[1,16,128,256]{3,1,0,2:T(8,128)(2,1)S(1)}, u32[]{:S(2)}) copy-start(bf16[1,16,128,256]{3,1,0,2:T(8,128)(2,1)S(1)} %all-to-all-done) | copy-start | bytes 3145732
  246.5 37.3 %all-to-all-start.2 = ((bf16[1,16,128,256]{3,1,0,2:T(8,128)(2,1)}), bf16[1,16,128,256]{3,1,0,2:T(8,128)(2,1)}, u32[]{:S(2)}, u32[]{:S(2)}) async-start(bf16[1,16,128,256]{3,1,0,2:T(8,128)(2,1)} %copy.180), calls=%async_computation.2 | async-start | bytes 2097152 | tf_op jit(solution)/shard_map/all_to_all | solution.py:130
  250.7 230.2 %all-gather.7.cloned.1.call-start = ((), (), s32[]{:S(2)}) async-start(), calls=%async_computation.7 | async-start | bytes 23592960 | tf_op jit(solution)/shard_map/all_gather | solution.py:161
  270.1 6.9 %copy-start.16 = (bf16[1,16,128,256]{3,1,0,2:T(8,128)(2,1)S(1)}, bf16[1,16,128,256]{3,1,0,2:T(8,128)(2,1)}, u32[]{:S(2)}) copy-start(bf16[1,16,128,256]{3,1,0,2:T(8,128)(2,1)} %copy-done.15) | copy-start | bytes 3145732
  290.1 22.3 %copy-start.5 = (bf16[1,16,128,256]{2,3,1,0:T(8,128)(2,1)S(1)}, bf16[1,16,128,256]{2,3,1,0:T(8,128)(2,1)}, u32[]{:S(2)}) copy-start(bf16[1,16,128,256]{2,3,1,0:T(8,128)(2,1)} %copy.204) | copy-start | bytes 3145732
  362.7 175.4 %all-gather.11.cloned.1.call-start = ((), (), s32[]{:S(2)}) async-start(), calls=%async_computation.9 | async-start | bytes 2985984 | tf_op jit(solution)/shard_map/all_gather | solution.py:179
  363.5 230.2 %all-gather.9.cloned.1.call-start = ((), (), s32[]{:S(2)}) async-start(), calls=%async_computation.8 | async-start | bytes 2985984 | tf_op jit(solution)/shard_map/all_gather | solution.py:172
  364.0 294.7 %reduce-scatter.2.cloned.1.call-start = ((), (), s32[]{:S(2)}) async-start(), calls=%async_computation.10 | async-start | bytes 5898240 | tf_op jit(solution)/shard_map/reduce_scatter | solution.py:184
  (11 other events, 28.9 us)
Sparse Core Ops, SparseCore 0:
  8.9 40.1 all-gather.4
  362.8 118.0 all-gather.6
  483.1 54.9 all-gather.10
  540.1 53.5 all-gather.8
  612.2 46.4 reduce-scatter.1
